TPU v7x, 32 devices: a whole 2x2x4 slice. The times are simulated.
32 devices in a mesh: groups: 2 (over x), visit: 16 (over z, y, core).
Axes of the slice: x: 2, y: 2, z: 4, core: 2. Of those that a mesh axis runs over, the one named last changes fastest.
Arguments:
- visit_image: bfloat16 [32, 256, 1024], P(('groups', 'visit')), parts along dimension 0, may hold values from -6 to 6
- band_offset: int32 [32, 2], P(('groups', 'visit')), parts along dimension 0, may hold values from -8 to 8
- shift_frac: float32 [32, 2], P(('groups', 'visit')), parts along dimension 0, may hold values from 0 to 1
- weights: bfloat16 [32], P(('groups', 'visit')), parts along dimension 0, may hold values from 0.29882812 to 3
- box_owner: int32 [32, 128, 1], P(('groups', 'visit')), parts along dimension 0, may hold values from 0 to 15; in each aligned block of 128 rows (0 to 127, 128 to 255, ..., all dimensions but the last counted through in order) at most 16 rows name the same one
- box_slot: int32 [32, 128], P(('groups', 'visit')), parts along dimension 0, may hold values from 0 to 15
- basis_index: int32 [32, 6], P(('groups', 'visit')), parts along dimension 0, may hold values from 0 to 11
- basis_coef: float32 [32, 6], P(('groups', 'visit')), parts along dimension 0, may hold values from 0.1 to 0.3
- basis_width: float32 [12], replicated, may hold values from 0.7 to 4
Outputs:
- template_coadd: bfloat16 [512, 16, 128], P(('groups', 'visit')), parts along dimension 0
- difference_coadd: float32 [512, 16, 128], P(('groups', 'visit')), parts along dimension 0
There are 2 independent parts, one for each index of `groups`. A program takes and returns all parts, laid end to end along the dimension named above; an argument that names none is the same for every part. Nothing has to cross between parts.
Inputs may be any that keep to these rules, and one draw needn't show every extreme that they name: `box_owner`: among the 128 boxes of one visit no owner is named more than 16 times, and in every draw some visit names some owner exactly 16 times.
All inputs are finite; a program needn't handle non-finite values.
Results may differ from a plain program's by a relative error of at most 0.012.
The roundings to bfloat16 on the way count: a program that leaves them out, or rounds other values in their place, can miss the bound.
Values may be sent and summed in bfloat16 or wider, within the bound.
A program may use at most 64 MiB of HBM per device.

v0:
```python
import jax
import jax.numpy as jnp
from jax import lax
from jax.sharding import PartitionSpec as P

BH = 16
BW = 128
PS = 16


band_reach = 8.0


def lanczos_band(extent, shift_by, by_rows):
    out_index = jnp.arange(extent, dtype=jnp.float32)[:, None]
    in_index = jnp.arange(extent, dtype=jnp.float32)[None, :]
    if by_rows:
        offset = in_index - out_index - shift_by
    else:
        offset = out_index - in_index - shift_by
    kernel_value = jnp.sinc(offset) * jnp.sinc(offset / 3.0)
    return jnp.where(jnp.abs(offset) < 3.0, kernel_value, 0.0).astype(jnp.bfloat16)


def gauss_band(extent, blur_width):
    out_index = jnp.arange(extent, dtype=jnp.float32)[:, None]
    in_index = jnp.arange(extent, dtype=jnp.float32)[None, :]
    pixel_gap = out_index - in_index
    tap_offsets = jnp.arange(17, dtype=jnp.float32) - 8.0
    spread = 2.0 * blur_width * blur_width
    tap_total = jnp.sum(jnp.exp(-tap_offsets * tap_offsets / spread))
    kernel_value = jnp.where(
        jnp.abs(pixel_gap) <= band_reach, jnp.exp(-pixel_gap * pixel_gap / spread), 0.0
    )
    return (kernel_value / tap_total).astype(jnp.bfloat16)


def to_boxes(picture, box_rows, box_cols):
    pix_rows, pix_cols = picture.shape
    split = picture.reshape(pix_rows // box_rows, box_rows, pix_cols // box_cols, box_cols)
    return split.transpose(0, 2, 1, 3).reshape(-1, box_rows * box_cols)


def from_boxes(flat_boxes, pix_rows, pix_cols, box_rows, box_cols):
    split = flat_boxes.reshape(pix_rows // box_rows, pix_cols // box_cols, box_rows, box_cols)
    return split.transpose(0, 2, 1, 3).reshape(pix_rows, pix_cols)


def tag_product(tag_rows, box_data):
    return lax.dot_general(
        tag_rows, box_data, (((0,), (0,)), ((), ())), preferred_element_type=jnp.float32
    )


def shards(
    visit_image,
    band_offset,
    shift_frac,
    weights,
    box_owner,
    box_slot,
    basis_index,
    basis_coef,
    basis_width,
):
    picture = visit_image[0]
    pix_rows, pix_cols = picture.shape
    shifts = band_offset[0].astype(jnp.float32) + shift_frac[0]
    row_warp = lanczos_band(pix_rows, shifts[0], True)
    col_warp = lanczos_band(pix_cols, shifts[1], False)
    col_pass = jnp.dot(picture, col_warp, preferred_element_type=jnp.float32).astype(jnp.bfloat16)
    warped = jnp.dot(row_warp, col_pass, preferred_element_type=jnp.float32).astype(jnp.bfloat16)
    box_data = to_boxes(warped, BH, BW)
    box_count = box_data.shape[0]
    peer_count = lax.axis_size("visit")
    capacity = max(2, 2 * box_count // peer_count)
    dest_ids = box_owner[0, :, 0]
    slot_ids = box_slot[0]
    dest_hits = (dest_ids[:, None] == jnp.arange(peer_count, dtype=jnp.int32)[None, :]).astype(
        jnp.int32
    )
    earlier = jnp.cumsum(dest_hits, axis=0) - dest_hits
    dest_rank = jnp.sum(earlier * dest_hits, axis=1)
    buffer_row = dest_ids * capacity + dest_rank
    visit_weight = weights[0]
    slot_hits = slot_ids[:, None] == jnp.arange(PS, dtype=jnp.int32)[None, :]
    tag_rows = jnp.where(slot_hits, visit_weight, jnp.zeros((), jnp.bfloat16))
    sent_boxes = (
        jnp.zeros((peer_count * capacity, box_data.shape[1]), jnp.bfloat16)
        .at[buffer_row]
        .set(box_data)
    )
    sent_tags = jnp.zeros((peer_count * capacity, PS), jnp.bfloat16).at[buffer_row].set(tag_rows)
    received, received_tags = (
        lax.all_to_all(sent_boxes, "visit", split_axis=0, concat_axis=0, tiled=True),
        lax.all_to_all(sent_tags, "visit", split_axis=0, concat_axis=0, tiled=True),
    )
    summed = tag_product(received_tags, received)
    weight_sum = 1.0 + jnp.sum(received_tags.astype(jnp.float32), axis=0)
    template = (summed / weight_sum[:, None]).astype(jnp.bfloat16)
    chosen = (received_tags > 0).astype(jnp.bfloat16)
    reply_rows = jnp.dot(chosen, template, preferred_element_type=jnp.float32).astype(jnp.bfloat16)
    came_back = lax.all_to_all(reply_rows, "visit", split_axis=0, concat_axis=0, tiled=True)
    returned_boxes = came_back[buffer_row]
    template_image = from_boxes(returned_boxes, pix_rows, pix_cols, BH, BW)
    basis_ids = jnp.arange(basis_width.shape[0], dtype=jnp.int32)
    matched = jnp.zeros((pix_rows, pix_cols), jnp.float32)
    for member in range(basis_index.shape[1]):
        blur_width = jnp.sum(jnp.where(basis_ids == basis_index[0, member], basis_width, 0.0))
        across = gauss_band(pix_cols, blur_width)
        down_band = gauss_band(pix_rows, blur_width)
        blurred = jnp.dot(template_image, across, preferred_element_type=jnp.float32).astype(
            jnp.bfloat16
        )
        matched = matched + basis_coef[0, member] * jnp.dot(
            down_band, blurred, preferred_element_type=jnp.float32
        )
    difference = (warped.astype(jnp.float32) - matched).astype(jnp.bfloat16)
    diff_boxes = to_boxes(difference, BH, BW)
    sent_diff = (
        jnp.zeros((peer_count * capacity, diff_boxes.shape[1]), jnp.bfloat16)
        .at[buffer_row]
        .set(diff_boxes)
    )
    received_diff = lax.all_to_all(sent_diff, "visit", split_axis=0, concat_axis=0, tiled=True)
    difference_coadd = tag_product(received_tags, received_diff) / weight_sum[:, None]
    return (template.reshape(PS, BH, BW), difference_coadd.reshape(PS, BH, BW))


def solution(mesh):
    placed = (
        P(("groups", "visit"), None, None),
        P(("groups", "visit"), None),
        P(("groups", "visit"), None),
        P(("groups", "visit")),
        P(("groups", "visit"), None, None),
        P(("groups", "visit"), None),
        P(("groups", "visit"), None),
        P(("groups", "visit"), None),
        P(),
    )
    return jax.shard_map(
        shards,
        mesh=mesh,
        in_specs=placed,
        out_specs=(P(("groups", "visit"), None, None), P(("groups", "visit"), None, None)),
        check_vma=False,
    )
```

profile of v0, /device:TPU:0, one launch (start us, length us, event | category | flops | bytes accessed | tf_op | source)
XLA Modules:
  0.0 153.0 jit_solution(590456195435126809)
XLA Ops:
  0.6 0.0 copy-start
  0.6 0.8 fusion.171
  1.4 0.2 reduce_window_sum.11
  1.6 0.8 select_reduce_fusion
  2.4 0.7 fusion.185
  3.8 1.1 scatter_custom_fusion
  4.9 0.1 copy.14
  5.0 0.7 reshape.125
  5.7 7.4 %all-to-all-start = ((bf16[16,2,128]{2,1,0:T(2,128)(2,1)}), bf16[16,2,128]{2,1,0:T(2,128)(2,1)S(1)}, u32[]{:S(2)}, u32[]{:S(2)}) async-start(bf16[16,2,128]{2,1,0:T(2,128)(2,1)} %reshape.125), calls=%async_computation | async-start | bytes 16384 | tf_op jit(solution)/shard_map/all_to_all | solution.py:96
  13.1 0.7 convert_add_fusion
  13.8 0.7 fusion.238
  14.5 12.7 %convolution_convert_fusion.1 = bf16[256,1024]{1,0:T(8,128)(2,1)S(1)} fusion(f32[]{:T(128)} %bitcast.8, bf16[1,256,1024]{2,1,0:T(8,128)(2,1)S(1)} %copy-done, f32[]{:T(128)} %bitcast.7), kind=kOutput, calls=%fused_computation.112 | convolution fusion | flops 752943104 | bytes 1048584 | tf_op jit(solution)/shard_map/dot_general | solution.py:72
  27.2 0.1 copy.18
  27.3 2.6 %scatter_custom_fusion.1 = bf16[256,2048]{1,0:T(8,128)(2,1)} fusion(s32[128]{0:T(128)S(1)} %fusion.185, bf16[]{:T(256)} %constant.11.clone.1, bf16[16,16,8,128]{3,2,1,0:T(8,128)(2,1)S(1)} %bitcast.117), kind=kCustom, calls=%fused_computation.126 | custom fusion | bytes 1572866 | tf_op jit(solution)/shard_map/scatter | solution.py:91
  29.9 0.0 all-to-all-done
  29.9 6.0 %all-to-all-start.1 = ((bf16[16,16,2048]{2,1,0:T(8,128)(2,1)}), bf16[16,16,2048]{2,1,0:T(8,128)(2,1)S(1)}, u32[]{:S(2)}, u32[]{:S(2)}) async-start(bf16[16,16,2048]{2,1,0:T(8,128)(2,1)} %bitcast.12), calls=%async_computation.1 | async-start | bytes 2097152 | tf_op jit(solution)/shard_map/all_to_all | solution.py:95
  35.9 0.1 reshape.126
  36.1 0.1 gt.7
  36.2 0.1 convert_reduce_fusion
  36.4 22.5 %all-to-all-done.1 = bf16[16,16,2048]{2,1,0:T(8,128)(2,1)S(1)} async-done(((bf16[16,16,2048]{2,1,0:T(8,128)(2,1)}), bf16[16,16,2048]{2,1,0:T(8,128)(2,1)S(1)}, u32[]{:S(2)}, u32[]{:S(2)}) %all-to-all-start.1) | async-done | bytes 1048608 | tf_op jit(solution)/shard_map/all_to_all | solution.py:95
  58.8 0.4 fusion.33
  59.3 1.5 convolution_convert_fusion
  60.7 6.9 %all-to-all-start.2 = ((bf16[16,16,2048]{2,1,0:T(8,128)(2,1)}), bf16[16,16,2048]{2,1,0:T(8,128)(2,1)S(1)}, u32[]{:S(2)}, u32[]{:S(2)}) async-start(bf16[16,16,2048]{2,1,0:T(8,128)(2,1)} %bitcast.16), calls=%async_computation.2 | async-start | bytes 2097152 | tf_op jit(solution)/shard_map/all_to_all | solution.py:103
  67.7 0.0 copy-done.1
  67.7 0.7 fusion.237
  68.4 4.5 %fusion.184 = (f32[]{:T(128)}, f32[]{:T(128)}, f32[]{:T(128)}, f32[]{:T(128)}, f32[]{:T(128)}, /*index=5*/f32[]{:T(128)}) fusion(f32[12]{0:T(128)S(1)} %copy-done.3, s32[]{:T(128)} %bitcast.29, s32[]{:T(128)} %bitcast.25, s32[]{:T(128)} %bitcast.23, s32[]{:T(128)} %bitcast.21, s32[]{:T(128)} %bitcast.15, s32[]{:T(128)} %bitcast.27), kind=kLoop, calls=%fused_computation.257 | loop fusion | flops 210 | bytes 96 | tf_op jit(solution)/shard_map/reduce_sum | solution.py:109
  80.3 0.6 exponential_reduce_fusion.5
  80.9 0.7 exponential_reduce_fusion.4
  81.6 0.7 exponential_reduce_fusion.3
  82.3 0.6 exponential_reduce_fusion.2
  82.9 0.6 exponential_reduce_fusion.1
  83.6 0.7 exponential_reduce_fusion
  84.3 0.7 fusion.236
  84.9 5.6 %all-to-all-done.2 = bf16[16,16,2048]{2,1,0:T(8,128)(2,1)S(1)} async-done(((bf16[16,16,2048]{2,1,0:T(8,128)(2,1)}), bf16[16,16,2048]{2,1,0:T(8,128)(2,1)S(1)}, u32[]{:S(2)}, u32[]{:S(2)}) %all-to-all-start.2) | async-done | bytes 1048608 | tf_op jit(solution)/shard_map/all_to_all | solution.py:103
  90.6 0.9 gather_fusion
  91.5 4.5 %convolution_multiply_fusion.5 = f32[256,1024]{1,0:T(8,128)} fusion(f32[]{:T(128)} %exponential_reduce_fusion.5, f32[]{:T(128)S(6)} %mul.256, f32[]{:T(128)} %bitcast.14, bf16[32,8,8,128]{3,2,1,0:T(8,128)(2,1)S(1)} %bitcast.118), kind=kOutput, calls=%fused_computation.105 | convolution fusion | flops 681639936 | bytes 1572876 | tf_op jit(solution)/shard_map/dot_general | solution.py:115
  96.0 4.8 %fusion.62 = f32[256,1024]{1,0:T(8,128)S(1)} fusion(f32[256,1024]{1,0:T(8,128)} %convolution_multiply_fusion.5, f32[]{:T(128)} %exponential_reduce_fusion.4, f32[]{:T(128)S(6)} %mul.262, f32[]{:T(128)} %bitcast.20, bf16[32,8,8,128]{3,2,1,0:T(8,128)(2,1)S(1)} %bitcast.119), kind=kOutput, calls=%fused_computation.104 | convolution fusion | flops 681902080 | bytes 2621452 | tf_op jit(solution)/shard_map/dot_general | solution.py:115
  100.9 4.5 %fusion.61 = f32[256,1024]{1,0:T(8,128)} fusion(f32[256,1024]{1,0:T(8,128)S(1)} %fusion.62, f32[]{:T(128)} %exponential_reduce_fusion.3, f32[]{:T(128)S(6)} %mul.266, f32[]{:T(128)} %bitcast.22, bf16[32,8,8,128]{3,2,1,0:T(8,128)(2,1)S(1)} %bitcast.120), kind=kOutput, calls=%fused_computation.102 | convolution fusion | flops 681902080 | bytes 2621452 | tf_op jit(solution)/shard_map/dot_general | solution.py:115
  105.4 4.8 %fusion.60 = f32[256,1024]{1,0:T(8,128)S(1)} fusion(f32[256,1024]{1,0:T(8,128)} %fusion.61, f32[]{:T(128)} %exponential_reduce_fusion.2, f32[]{:T(128)S(6)} %mul.270, f32[]{:T(128)} %bitcast.24, bf16[32,8,8,128]{3,2,1,0:T(8,128)(2,1)S(1)} %bitcast.121), kind=kOutput, calls=%fused_computation.100 | convolution fusion | flops 681902080 | bytes 2621452 | tf_op jit(solution)/shard_map/dot_general | solution.py:115
  110.2 4.4 %fusion.59 = f32[256,1024]{1,0:T(8,128)} fusion(f32[256,1024]{1,0:T(8,128)S(1)} %fusion.60, f32[]{:T(128)} %exponential_reduce_fusion.1, f32[]{:T(128)S(6)} %mul.274, f32[]{:T(128)} %bitcast.26, bf16[32,8,8,128]{3,2,1,0:T(8,128)(2,1)S(1)} %bitcast.122), kind=kOutput, calls=%fused_computation.98 | convolution fusion | flops 681902080 | bytes 2621452 | tf_op jit(solution)/shard_map/dot_general | solution.py:115
  114.6 5.1 %fusion.73 = bf16[32,8,8,128]{3,1,2,0:T(8,128)(2,1)S(1)} fusion(f32[256,1024]{1,0:T(8,128)} %fusion.59, bf16[256,1024]{1,0:T(8,128)(2,1)S(1)} %convolution_convert_fusion.1, f32[]{:T(128)} %exponential_reduce_fusion, f32[]{:T(128)S(6)} %mul.278, f32[]{:T(128)} %bitcast.28, bf16[32,8,8,128]{3,2,1,0:T(8,128)(2,1)S(1)} %bitcast.123), kind=kOutput, calls=%fused_computation.115 | convolution fusion | flops 682688512 | bytes 2621452 | tf_op jit(solution)/shard_map/dot_general | solution.py:115
  119.7 0.1 copy.21
  119.8 2.5 %scatter_custom_fusion.2 = bf16[256,2048]{1,0:T(8,128)(2,1)} fusion(s32[128]{0:T(128)S(1)} %fusion.185, bf16[]{:T(256)} %constant.11.clone.1, bf16[16,16,8,128]{3,2,1,0:T(8,128)(2,1)S(1)} %bitcast.116), kind=kCustom, calls=%fused_computation.118 | custom fusion | bytes 1572866 | tf_op jit(solution)/shard_map/scatter | solution.py:123
  122.2 6.8 %all-to-all-start.3 = ((bf16[16,16,2048]{2,1,0:T(8,128)(2,1)}), bf16[16,16,2048]{2,1,0:T(8,128)(2,1)S(1)}, u32[]{:S(2)}, u32[]{:S(2)}) async-start(bf16[16,16,2048]{2,1,0:T(8,128)(2,1)} %bitcast.32), calls=%async_computation.3 | async-start | bytes 2097152 | tf_op jit(solution)/shard_map/all_to_all | solution.py:125
  129.0 0.6 copy.19
  129.7 22.2 %all-to-all-done.3 = bf16[16,16,2048]{2,1,0:T(8,128)(2,1)S(1)} async-done(((bf16[16,16,2048]{2,1,0:T(8,128)(2,1)}), bf16[16,16,2048]{2,1,0:T(8,128)(2,1)S(1)}, u32[]{:S(2)}, u32[]{:S(2)}) %all-to-all-start.3) | async-done | bytes 1048608 | tf_op jit(solution)/shard_map/all_to_all | solution.py:125
  151.9 0.4 fusion.76
  152.3 0.7 copy.22
  (10 shorter events, 0.1 us)
Async XLA Ops:
  0.6 13.8 %copy-start = (bf16[1,256,1024]{2,1,0:T(8,128)(2,1)S(1)}, bf16[1,256,1024]{2,1,0:T(8,128)(2,1)}, u32[]{:S(2)}) copy-start(bf16[1,256,1024]{2,1,0:T(8,128)(2,1)} %param.11) | copy-start | bytes 1572868
  5.7 24.2 %all-to-all-start = ((bf16[16,2,128]{2,1,0:T(2,128)(2,1)}), bf16[16,2,128]{2,1,0:T(2,128)(2,1)S(1)}, u32[]{:S(2)}, u32[]{:S(2)}) async-start(bf16[16,2,128]{2,1,0:T(2,128)(2,1)} %reshape.125), calls=%async_computation | async-start | bytes 16384 | tf_op jit(solution)/shard_map/all_to_all | solution.py:96
  29.9 28.9 %all-to-all-start.1 = ((bf16[16,16,2048]{2,1,0:T(8,128)(2,1)}), bf16[16,16,2048]{2,1,0:T(8,128)(2,1)S(1)}, u32[]{:S(2)}, u32[]{:S(2)}) async-start(bf16[16,16,2048]{2,1,0:T(8,128)(2,1)} %bitcast.12), calls=%async_computation.1 | async-start | bytes 2097152 | tf_op jit(solution)/shard_map/all_to_all | solution.py:95
  60.7 6.9 %copy-start.1 = (s32[1,6]{1,0:T(1,128)S(1)}, s32[1,6]{1,0:T(1,128)}, u32[]{:S(2)}) copy-start(s32[1,6]{1,0:T(1,128)} %param.17) | copy-start | bytes 76
  60.7 7.6 %copy-start.3 = (f32[12]{0:T(128)S(1)}, f32[12]{0:T(128)}, u32[]{:S(2)}) copy-start(f32[12]{0:T(128)} %param.19) | copy-start | bytes 148
  60.7 23.5 %copy-start.2 = (f32[1,6]{1,0:T(1,128)S(1)}, f32[1,6]{1,0:T(1,128)}, u32[]{:S(2)}) copy-start(f32[1,6]{1,0:T(1,128)} %param.18) | copy-start | bytes 76
  60.7 29.8 %all-to-all-start.2 = ((bf16[16,16,2048]{2,1,0:T(8,128)(2,1)}), bf16[16,16,2048]{2,1,0:T(8,128)(2,1)S(1)}, u32[]{:S(2)}, u32[]{:S(2)}) async-start(bf16[16,16,2048]{2,1,0:T(8,128)(2,1)} %bitcast.16), calls=%async_computation.2 | async-start | bytes 2097152 | tf_op jit(solution)/shard_map/all_to_all | solution.py:103
  122.2 29.7 %all-to-all-start.3 = ((bf16[16,16,2048]{2,1,0:T(8,128)(2,1)}), bf16[16,16,2048]{2,1,0:T(8,128)(2,1)S(1)}, u32[]{:S(2)}, u32[]{:S(2)}) async-start(bf16[16,16,2048]{2,1,0:T(8,128)(2,1)} %bitcast.32), calls=%async_computation.3 | async-start | bytes 2097152 | tf_op jit(solution)/shard_map/all_to_all | solution.py:125
where the time goes:
time: 155 us; the launch traced here: 153 us
  waiting for transfers between devices  50.4 us (33%)
  matrix products  43.2 us (28%)
  starting transfers between devices  27.1 us (17%)
  other arithmetic  12.8 us (8%)
  local copies, waits for them, and re-layouts  10.6 us (7%)
  between operations  8.94 us (6%)
    dot_general x6, matrix products, shards(): jnp.dot(down_band, blurred, preferred_element_type=jnp.float32)  28.2 us
    all_to_all x1, waiting for transfers between devices, shards(): lax.all_to_all(sent_boxes, 'visit', split_axis=0, concat_axis=0, tiled=True)  22.5 us
    all_to_all x1, waiting for transfers between devices, shards(): lax.all_to_all(sent_diff, 'visit', split_axis=0, concat_axis=0, tiled=True)  22.2 us
    dot_general x1, matrix products, shards(): jnp.dot(row_warp, col_pass, preferred_element_type=jnp.float32)  12.7 us
    all_to_all x1, starting transfers between devices, shards(): lax.all_to_all(sent_tags, 'visit', split_axis=0, concat_axis=0, tiled=True)  7.41 us
    all_to_all x1, starting transfers between devices, shards(): lax.all_to_all(reply_rows, 'visit', split_axis=0, concat_axis=0, tiled=True)  6.92 us
    all_to_all x1, starting transfers between devices, shards(): lax.all_to_all(sent_diff, 'visit', split_axis=0, concat_axis=0, tiled=True)  6.79 us
    all_to_all x1, starting transfers between devices, shards(): lax.all_to_all(sent_boxes, 'visit', split_axis=0, concat_axis=0, tiled=True)  6.01 us
  transfers between devices with their start and end apart: 4, of which 3 were waited for; matrix products, arithmetic and copies ran while one was open for 18% of the time, Pallas kernels for 0%

commit v1 on v0

--- a/solution.py
+++ b/solution.py
@@ -1,11 +1,17 @@
+import functools
+import math
+
 import jax
 import jax.numpy as jnp
 from jax import lax
+from jax.experimental import pallas as pl
+from jax.experimental.pallas import tpu as pltpu
 from jax.sharding import PartitionSpec as P
 
 BH = 16
 BW = 128
 PS = 16
+CHUNKS = 4
 
 
 band_reach = 8.0
@@ -127,6 +133,463 @@
     return (template.reshape(PS, BH, BW), difference_coadd.reshape(PS, BH, BW))
 
 
+MESH = pl.DeviceIdType.MESH
+
+
+def sinc_of(x):
+    angle = jnp.float32(math.pi) * x
+    safe = jnp.where(x == 0.0, 1.0, angle)
+    return jnp.where(x == 0.0, 1.0, jnp.sin(safe) / safe)
+
+
+def lanczos_of(x):
+    return jnp.where(jnp.abs(x) < 3.0, sinc_of(x) * sinc_of(x / 3.0), 0.0)
+
+
+def iota(shape, axis):
+    return lax.broadcasted_iota(jnp.int32, shape, axis)
+
+
+def one_hot(hit):
+    return jnp.where(hit, 1.0, 0.0).astype(jnp.bfloat16)
+
+
+def dot32(left, right):
+    return jnp.dot(left, right, preferred_element_type=jnp.float32)
+
+
+def dense_kernel(
+    peers,
+    chunks,
+    params,
+    basis_ids,
+    widths,
+    image,
+    target,
+    template_out,
+    diff_out,
+    col_pass,
+    warped,
+    row_warp,
+    tag_rows,
+    pick_rows,
+    across_all,
+    down_all,
+    blurred,
+    keep_weight,
+    send_weight,
+    recv_weight,
+    keep0,
+    keep1,
+    keep2,
+    send0,
+    recv0,
+    send1,
+    recv1,
+    send2,
+    recv2,
+    gathered,
+    matched,
+    weight_sems,
+    sems0,
+    sems1,
+    sems2,
+    gather_sems,
+):
+    bf16 = jnp.bfloat16
+    f32 = jnp.float32
+    depth = peers // 4
+    rows, cols = image.shape[1:]
+    box_rows, box_cols = rows // BH, cols // BW
+    boxes = box_rows * box_cols
+    slots = peers * PS
+    members = basis_ids.shape[1]
+    width = BH * BW // chunks
+    per = BH // chunks
+    band_rows = per * box_rows
+    me = lax.axis_index("visit")
+    core = lax.rem(me, 2)
+    side = lax.rem(lax.div(me, 2), 2)
+    layer = lax.div(me, 4)
+
+    def device_at(d, other_side, other_core):
+        there = lax.rem(layer + d, depth)
+        s = 1 - side if other_side else side
+        c = 1 - core if other_core else core
+        return {"visit": (there * 2 + s) * 2 + c}
+
+    def block_at(q):
+        a, b, d = q // (2 * depth), (q // depth) % 2, q % depth
+        return device_at(d, b == 0, a == 0)
+
+    own = 3 * depth
+    barrier = pltpu.get_barrier_semaphore()
+    for q in range(peers):
+        if q != own:
+            pl.semaphore_signal(barrier, inc=1, device_id=block_at(q), device_id_type=MESH)
+
+    row_id = iota((slots, boxes), 0)
+    block = lax.div(row_id, PS)
+    a = lax.div(block, 2 * depth)
+    b = lax.rem(lax.div(block, depth), 2)
+    d = lax.rem(block, depth)
+    owner = (
+        lax.rem(layer + d, depth) * 2 + lax.rem(side + 1 - b, 2)
+    ) * 2 + lax.rem(core + 1 - a, 2)
+    hits = one_hot(owner * PS + lax.rem(row_id, PS) == target[...])
+    k_row = iota((boxes, boxes), 0)
+    k_col = iota((boxes, boxes), 1)
+    order_of = lambda k: lax.rem(k, box_rows) * box_cols + lax.div(k, box_rows)
+    sorter = one_hot(k_row == order_of(k_col))
+    sorter_t = one_hot(order_of(k_row) == k_col)
+    visit_weight = params[0, 2]
+    tags = dot32(hits, sorter) * visit_weight
+    tag_rows[...] = tags.astype(bf16)
+    pick_rows[...] = lax.dot_general(
+        sorter_t, hits, (((1,), (1,)), ((), ())), preferred_element_type=f32
+    ).astype(bf16)
+    totals = dot32(tag_rows[...], jnp.ones((boxes, BW), bf16))
+    for q in range(peers):
+        if q == own:
+            keep_weight[...] = totals[q * PS : (q + 1) * PS, :]
+        else:
+            send_weight[q] = totals[q * PS : (q + 1) * PS, :]
+
+    half = BW // 2
+    window = 2 * BW
+    lane = iota((8, window), 1)
+    col_taps = lanczos_of((window - half - lane).astype(f32) - params[0, 1])
+    col_table = pltpu.roll(
+        jnp.broadcast_to(col_taps[:1], (window, window)), 0, 1, stride=1, stride_axis=0
+    )[:, :BW].astype(bf16)
+    lane = iota((8, rows), 1)
+    gap = jnp.where(lane < rows // 2, lane, lane - rows)
+    row_taps = lanczos_of(gap.astype(f32) - params[0, 0])
+    row_table = pltpu.roll(
+        jnp.broadcast_to(row_taps[:1], (rows, rows)), 0, 1, stride=1, stride_axis=0
+    )
+    i_row = iota((rows, rows), 0)
+    i_col = iota((rows, rows), 1)
+    row_table = jnp.where(jnp.abs(i_col - i_row) < rows // 2, row_table, 0.0).astype(bf16)
+    place = lambda r: lax.rem(r, box_rows) * BH + lax.div(r, box_rows)
+    row_warp[...] = dot32(one_hot(place(i_row) == i_col), row_table).astype(bf16)
+
+    def windows(picture):
+        edge = jnp.zeros((picture.shape[0], half), bf16)
+        padded = jnp.concatenate([edge, picture, edge], axis=1)
+        return jnp.concatenate(
+            [padded[:, j * BW : j * BW + window] for j in range(box_cols)], axis=0
+        )
+
+    step = rows // 4
+    for part in range(4):
+        here = slice(part * step, (part + 1) * step)
+        passed = dot32(windows(image[0, here, :]), col_table).astype(bf16)
+        for j in range(box_cols):
+            col_pass[here, j * BW : (j + 1) * BW] = passed[j * step : (j + 1) * step]
+
+    def to_slots(picture):
+        tiles = jnp.concatenate(
+            [
+                jnp.concatenate(
+                    [
+                        picture[r * box_rows : (r + 1) * box_rows, j * BW : (j + 1) * BW]
+                        for j in range(box_cols)
+                    ],
+                    axis=0,
+                )
+                for r in range(per)
+            ],
+            axis=1,
+        )
+        return dot32(tag_rows[...], tiles)
+
+    half0, half1 = slots // 2, slots // 4
+    pair = device_at(0, False, True)
+    across_y = device_at(0, True, False)
+
+    def copy0(turn, ch):
+        return pltpu.make_async_remote_copy(
+            send0.at[turn, ch], recv0.at[turn, ch], sems0.at[0, turn, ch], sems0.at[1, turn, ch],
+            device_id=pair, device_id_type=MESH,
+        )
+
+    def copy1(turn, ch):
+        return pltpu.make_async_remote_copy(
+            send1.at[turn, ch], recv1.at[turn, ch], sems1.at[0, turn, ch], sems1.at[1, turn, ch],
+            device_id=across_y, device_id_type=MESH,
+        )
+
+    def copy2(turn, ch, d):
+        return pltpu.make_async_remote_copy(
+            send2.at[turn, ch, d - 1],
+            recv2.at[turn, ch, d - 1],
+            sems2.at[0, turn, ch, d - 1],
+            sems2.at[1, turn, ch, d - 1],
+            device_id=device_at(d, False, False),
+            device_id_type=MESH,
+        )
+
+    def open_chunk(turn, ch, picture):
+        sums = to_slots(picture)
+        send0[turn, ch] = sums[:half0].astype(bf16)
+        keep0[ch] = sums[half0:]
+        copy0(turn, ch).start()
+
+    def middle(turn):
+        for ch in range(chunks):
+            copy0(turn, ch).wait_recv()
+            sums = keep0[ch] + recv0[turn, ch].astype(f32)
+            send1[turn, ch] = sums[:half1].astype(bf16)
+            keep1[ch] = sums[half1:]
+            copy1(turn, ch).start()
+        for ch in range(chunks):
+            copy1(turn, ch).wait_recv()
+            sums = keep1[ch] + recv1[turn, ch].astype(f32)
+            for d in range(1, depth):
+                send2[turn, ch, d - 1] = sums[d * PS : (d + 1) * PS].astype(bf16)
+            keep2[ch] = sums[:PS]
+            for d in range(1, depth):
+                copy2(turn, ch, d).start()
+
+    def close_chunk(turn, ch):
+        sums = keep2[ch]
+        for d in range(1, depth):
+            copy2(turn, ch, d).wait_recv()
+            sums = sums + recv2[turn, ch, d - 1].astype(f32)
+        return sums
+
+    def finish(turn):
+        for ch in range(chunks):
+            copy0(turn, ch).wait_send()
+            copy1(turn, ch).wait_send()
+            for d in range(1, depth):
+                copy2(turn, ch, d).wait_send()
+
+    def weight_copy(q):
+        return pltpu.make_async_remote_copy(
+            send_weight.at[q], recv_weight.at[q], weight_sems.at[0, q], weight_sems.at[1, q],
+            device_id=block_at(q), device_id_type=MESH,
+        )
+
+    pl.semaphore_wait(barrier, peers - 1)
+    for q in range(peers):
+        if q != own:
+            weight_copy(q).start()
+    for ch in range(chunks):
+        here = slice(ch * band_rows, (ch + 1) * band_rows)
+        warped[here, :] = dot32(row_warp[here, :], col_pass[...]).astype(bf16)
+        open_chunk(0, ch, warped[here, :])
+
+    across_gap = (iota((window, BW), 0) - iota((window, BW), 1) - half).astype(f32)
+    down_gap = (place(i_row) - place(i_col)).astype(f32)
+    tap = (iota((8, BW), 1) - 8).astype(f32)
+    def tables(member):
+        spread = jnp.full((1, BW), 2.0 * widths[basis_ids[0, member]] * widths[basis_ids[0, member]])
+        whole = jnp.sum(
+            jnp.where(tap <= 8.0, jnp.exp(-tap * tap / spread), 0.0), axis=1, keepdims=True
+        )[:1]
+        scale = spread[:, :1]
+
+        def value(gap):
+            near = jnp.where(jnp.abs(gap) <= band_reach, jnp.exp(-gap * gap / scale), 0.0)
+            return (near / whole).astype(bf16)
+
+        across_all[:, member * BW : (member + 1) * BW] = value(across_gap)
+        down_all[member] = value(down_gap)
+
+    for member in range(members):
+        tables(member)
+
+    middle(0)
+    weight_sum = 1.0 + keep_weight[...]
+    for q in range(peers):
+        if q != own:
+            weight_copy(q).wait_recv()
+            weight_sum = weight_sum + recv_weight[q]
+    wide_sum = jnp.concatenate([weight_sum] * per, axis=1)
+
+    def gather_copy(kind, ch, src, dst, where):
+        return pltpu.make_async_remote_copy(
+            gathered.at[ch, src],
+            gathered.at[ch, dst],
+            gather_sems.at[0, ch, kind],
+            gather_sems.at[1, ch, kind],
+            device_id=where,
+            device_id_type=MESH,
+        )
+
+    def along_z(ch, d):
+        return gather_copy(depth - d, ch, own, own + depth - d, device_at(d, False, False))
+
+    def along_y(ch, e):
+        return gather_copy(depth + e, ch, own + e, 2 * depth + e, across_y)
+
+    def along_core(ch, e):
+        return gather_copy(2 * depth + e, ch, 2 * depth + e, e, pair)
+
+    near_first = [e for e in (1, depth - 1)] + [e for e in range(2, depth - 1)]
+    if depth == 2:
+        near_first = [1]
+    for ch in range(chunks):
+        block = (close_chunk(0, ch) / wide_sum).astype(bf16)
+        template_out[:, ch * width : (ch + 1) * width] = block
+        gathered[ch, own] = block
+        for d in range(1, depth):
+            along_z(ch, d).start()
+        along_y(ch, 0).start()
+        along_core(ch, depth).start()
+    for ch in range(chunks):
+        for e in near_first:
+            along_z(ch, depth - e).wait_recv()
+            along_y(ch, e).start()
+            along_core(ch, depth + e).start()
+        along_y(ch, 0).wait_recv()
+        along_core(ch, 0).start()
+    for ch in range(chunks):
+        for e in near_first:
+            along_y(ch, e).wait_recv()
+            along_core(ch, e).start()
+    for ch in range(chunks):
+        for e in range(2 * depth):
+            along_core(ch, e).wait_recv()
+        flat = gathered[ch].reshape(slots, width)
+        picked = dot32(pick_rows[...], flat).astype(bf16)
+        picture = jnp.concatenate(
+            [
+                jnp.concatenate(
+                    [
+                        picked[j * box_rows : (j + 1) * box_rows, r * BW : (r + 1) * BW]
+                        for j in range(box_cols)
+                    ],
+                    axis=1,
+                )
+                for r in range(per)
+            ],
+            axis=0,
+        )
+        smeared = dot32(windows(picture), across_all[...]).astype(bf16)
+        for member in range(members):
+            for j in range(box_cols):
+                blurred[
+                    member, ch * band_rows : (ch + 1) * band_rows, j * BW : (j + 1) * BW
+                ] = smeared[
+                    j * band_rows : (j + 1) * band_rows, member * BW : (member + 1) * BW
+                ]
+
+    for j in range(0, cols, window):
+        total = jnp.zeros((rows, window), f32)
+        for member in range(members):
+            total = total + params[0, 3 + member] * dot32(
+                down_all[member], blurred[member, :, j : j + window]
+            )
+        matched[:, j : j + window] = (warped[:, j : j + window].astype(f32) - total).astype(bf16)
+
+    for ch in range(chunks):
+        open_chunk(1, ch, matched[ch * band_rows : (ch + 1) * band_rows, :])
+    middle(1)
+    for ch in range(chunks):
+        diff_out[:, ch * width : (ch + 1) * width] = close_chunk(1, ch) / wide_sum
+
+    finish(0)
+    finish(1)
+    for q in range(peers):
+        if q != own:
+            weight_copy(q).wait_send()
+    for ch in range(chunks):
+        for d in range(1, depth):
+            along_z(ch, d).wait_send()
+        for e in range(depth):
+            along_y(ch, e).wait_send()
+        for e in range(2 * depth):
+            along_core(ch, e).wait_send()
+
+
+def dense_shards(
+    visit_image,
+    band_offset,
+    shift_frac,
+    weights,
+    box_owner,
+    box_slot,
+    basis_index,
+    basis_coef,
+    basis_width,
+):
+    peers = lax.axis_size("visit")
+    depth = peers // 4
+    rows, cols = visit_image.shape[1:]
+    box_rows = rows // BH
+    boxes = box_rows * (cols // BW)
+    slots = peers * PS
+    members = basis_index.shape[1]
+    chunks = CHUNKS
+    width = BH * BW // chunks
+    bf16, f32 = jnp.bfloat16, jnp.float32
+    params = jnp.concatenate(
+        [
+            band_offset.astype(f32) + shift_frac,
+            weights.astype(f32)[None, :],
+            basis_coef,
+        ],
+        axis=1,
+    )
+    target = box_owner[:, :, 0] * PS + box_slot
+    smem = pl.BlockSpec(memory_space=pltpu.SMEM)
+    vmem = pl.BlockSpec(memory_space=pltpu.VMEM)
+    dma = pltpu.SemaphoreType.DMA
+    template, difference = pl.pallas_call(
+        functools.partial(dense_kernel, peers, chunks),
+        out_shape=(
+            jax.ShapeDtypeStruct((PS, BH * BW), bf16),
+            jax.ShapeDtypeStruct((PS, BH * BW), f32),
+        ),
+        in_specs=[smem, smem, smem, vmem, vmem],
+        out_specs=(vmem, vmem),
+        scratch_shapes=[
+            pltpu.VMEM((rows, cols), bf16),
+            pltpu.VMEM((rows, cols), bf16),
+            pltpu.VMEM((rows, rows), bf16),
+            pltpu.VMEM((slots, boxes), bf16),
+            pltpu.VMEM((boxes, slots), bf16),
+            pltpu.VMEM((2 * BW, members * BW), bf16),
+            pltpu.VMEM((members, rows, rows), bf16),
+            pltpu.VMEM((members, rows, cols), bf16),
+            pltpu.VMEM((PS, BW), f32),
+            pltpu.VMEM((peers, PS, BW), f32),
+            pltpu.VMEM((peers, PS, BW), f32),
+            pltpu.VMEM((chunks, slots // 2, width), f32),
+            pltpu.VMEM((chunks, slots // 4, width), f32),
+            pltpu.VMEM((chunks, PS, width), f32),
+            pltpu.VMEM((2, chunks, slots // 2, width), bf16),
+            pltpu.VMEM((2, chunks, slots // 2, width), bf16),
+            pltpu.VMEM((2, chunks, slots // 4, width), bf16),
+            pltpu.VMEM((2, chunks, slots // 4, width), bf16),
+            pltpu.VMEM((2, chunks, depth - 1, PS, width), bf16),
+            pltpu.VMEM((2, chunks, depth - 1, PS, width), bf16),
+            pltpu.VMEM((chunks, peers, PS, width), bf16),
+            pltpu.VMEM((rows, cols), bf16),
+            dma((2, peers)),
+            dma((2, 2, chunks)),
+            dma((2, 2, chunks)),
+            dma((2, 2, chunks, depth - 1)),
+            dma((2, chunks, 4 * depth)),
+        ],
+        compiler_params=pltpu.CompilerParams(collective_id=0, has_side_effects=True),
+    )(params, basis_index, basis_width, visit_image, target)
+    return (template.reshape(PS, BH, BW), difference.reshape(PS, BH, BW))
+
+
+def any_shards(*arrays):
+    peers = lax.axis_size("visit")
+    rows, cols = arrays[0].shape[1:]
+    boxes = (rows // BH) * (cols // BW)
+    capacity = max(2, 2 * boxes // peers)
+    if PS <= capacity and peers % 4 == 0 and peers >= 8 and rows == 2 * BW:
+        return dense_shards(*arrays)
+    return shards(*arrays)
+
+
 def solution(mesh):
     placed = (
         P(("groups", "visit"), None, None),
@@ -140,7 +603,7 @@
         P(),
     )
     return jax.shard_map(
-        shards,
+        any_shards,
         mesh=mesh,
         in_specs=placed,
         out_specs=(P(("groups", "visit"), None, None), P(("groups", "visit"), None, None)),

time: 155 us -> 54.5 us (0.35); the launches traced: 153 us -> 54.3 us
  waiting for transfers between devices: 50.4 us -> 0 us
  Pallas kernels: 0 us -> 48.3 us
  matrix products: 43.2 us -> 0 us
  starting transfers between devices: 27.1 us -> 0 us
  other arithmetic: 12.8 us -> 1.1 us
  between operations: 8.94 us -> 1.33 us
  local copies, waits for them, and re-layouts: 10.6 us -> 3.58 us
    all_to_all x4 -> x0, waiting for transfers between devices: 50.4 us -> none  [the longest x1 22.5 us: shards(): lax.all_to_all(sent_boxes, 'visit', split_axis=0, concat_axis=0, tiled=True)]
    pallas_call x0 -> x1, Pallas kernels: none -> 48.3 us  [dense_shards(): pl.pallas_call(functools.partial(dense_kernel, peers, chunks), out_shape=...]
    dot_general x10 -> x0, matrix products: 43.2 us -> none  [the longest x6 28.2 us: shards(): jnp.dot(down_band, blurred, preferred_element_type=jnp.float32)]
    all_to_all x4 -> x0, starting transfers between devices: 27.1 us -> none  [the longest x1 7.41 us: shards(): lax.all_to_all(sent_tags, 'visit', split_axis=0, concat_axis=0, tiled=True)]
    reduce_sum x9 -> x0, other arithmetic: 9.35 us -> none  [the longest x1 4.48 us: shards(): jnp.sum(jnp.where(basis_ids == basis_index[0, member], basis_width, 0.0))]
    scatter x2 -> x0, local copies, waits for them, and re-layouts: 5.1 us -> none  [the longest x1 2.64 us: shards(): sent_boxes = jnp.zeros((peer_count * capacity, box_data.shape[1]), jnp.bf...]
    slice x3 -> x0, local copies, waits for them, and re-layouts: 1.99 us -> none  [the longest x1 0.68 us: shards(): basis_index[0, member]]
  transfers between devices with their start and end apart: 4 -> 0, of which waited for: 3 -> 0; matrix products, arithmetic and copies ran while one was open for 18% -> 0% of each run, Pallas kernels for 0% -> 0%
where the time goes in v1:
time: 54.5 us; the launch traced here: 54.3 us
  Pallas kernels  48.3 us (89%)
  local copies, waits for them, and re-layouts  3.58 us (7%)
  between operations  1.33 us (2%)
  other arithmetic  1.1 us (2%)
    pallas_call x1, Pallas kernels, dense_shards(): pl.pallas_call(functools.partial(dense_kernel, peers, chunks), out_shape=...  48.3 us
    unnamed x14, local copies, waits for them, and re-layouts  3.58 us

profile of v1, /device:TPU:0, one launch (start us, length us, event | category | flops | bytes accessed | tf_op | source)
XLA Modules:
  0.0 54.3 jit_solution(3555460092074971288)
XLA Ops:
  1.3 0.0 copy-start.2
  1.3 0.0 copy-start.3
  1.3 0.6 %copy-done.2 = f32[1,2]{1,0:T(1,128)S(1)} copy-done((f32[1,2]{1,0:T(1,128)S(1)}, f32[1,2]{1,0:T(1,128)}, u32[]{:S(2)}) %copy-start.2) | copy-done | bytes 32
  1.9 0.0 copy-done.3
  2.0 0.0 copy-start.1
  2.0 0.6 %copy-done.1 = f32[1,6]{1,0:T(1,128)S(1)} copy-done((f32[1,6]{1,0:T(1,128)S(1)}, f32[1,6]{1,0:T(1,128)}, u32[]{:S(2)}) %copy-start.1) | copy-done | bytes 48
  2.6 0.0 copy-start.4
  2.6 0.0 copy-start.5
  2.6 0.6 %pad_maximum_fusion.params = f32[1,9]{1,0:T(1,128)} fusion(f32[1,6]{1,0:T(1,128)S(1)} %copy-done.1, f32[1,1]{1,0:T(1,128)S(6)} %convert.1, f32[1,2]{1,0:T(1,128)S(1)} %convert_add_fusion), kind=kLoop, calls=%fused_computation | loop fusion | flops 18 | bytes 72 | tf_op jit(solution)/shard_map/concatenate | solution.py:529
  3.2 0.1 copy-done.4
  3.3 0.0 copy-done.5
  3.3 0.5 bitcast_add_fusion.target
  3.8 48.3 %shard_map.104 = (bf16[16,2048]{1,0:T(8,128)(2,1)}, f32[16,2048]{1,0:T(8,128)}) custom-call(f32[1,9]{1,0:T(1,128)} %pad_maximum_fusion.params, s32[1,6]{1,0:T(1,128)} %basis_ids.1, f32[12]{0:T(128)} %widths.1, bf16[1,256,1024]{2,1,0:T(8,128)(2,1)} %image.1, s32[1,128]{1,0:T(1,128)} %bitcast_add_fusion.target), custom_call_target="tpu_custom_call" | custom-call | tf_op jit(solution)/shard_map/pallas_call | solution.py:541
  52.1 0.0 copy-start
  52.1 1.5 %copy.11 = bf16[2,8,16,128]{3,2,1,0:T(8,128)(2,1)} copy(bf16[2,8,16,128]{3,1,2,0:T(8,128)(2,1)} %bitcast.12) | data formatting | bytes 131072
  53.6 0.0 copy-done
  53.6 0.7 %copy.12 = f32[2,8,16,128]{3,2,1,0:T(8,128)} copy(f32[2,8,16,128]{3,1,2,0:T(8,128)S(1)} %bitcast.10) | data formatting | bytes 262144
  (1 shorter events, 0.0 us)
Async XLA Ops:
  1.3 0.7 %copy-start.2 = (f32[1,2]{1,0:T(1,128)S(1)}, f32[1,2]{1,0:T(1,128)}, u32[]{:S(2)}) copy-start(f32[1,2]{1,0:T(1,128)} %param.11) | copy-start | bytes 28
  1.3 0.7 %copy-start.3 = (s32[1,2]{1,0:T(1,128)S(1)}, s32[1,2]{1,0:T(1,128)}, u32[]{:S(2)}) copy-start(s32[1,2]{1,0:T(1,128)} %param.10) | copy-start | bytes 28
  2.0 0.7 %copy-start.1 = (f32[1,6]{1,0:T(1,128)S(1)}, f32[1,6]{1,0:T(1,128)}, u32[]{:S(2)}) copy-start(f32[1,6]{1,0:T(1,128)} %param.16) | copy-start | bytes 76
  2.6 0.7 %copy-start.4 = (s32[1,128]{1,0:T(1,128)S(1)}, s32[1,128]{1,0:T(1,128)}, u32[]{:S(2)}) copy-start(s32[1,128]{1,0:T(1,128)} %param.14) | copy-start | bytes 1540
  2.6 0.7 %copy-start.5 = (s32[1,128,1]{1,2,0:T(1,128)S(1)}, s32[1,128,1]{1,2,0:T(1,128)}, u32[]{:S(2)}) copy-start(s32[1,128,1]{1,2,0:T(1,128)} %param.13) | copy-start | bytes 1540
  52.1 1.5 %copy-start = (f32[16,2048]{1,0:T(8,128)S(1)}, f32[16,2048]{1,0:T(8,128)}, u32[]{:S(2)}) copy-start(f32[16,2048]{1,0:T(8,128)} %get-tuple-element.5) | copy-start | bytes 393220

commit v2 on v1

--- a/solution.py
+++ b/solution.py
@@ -150,6 +150,18 @@
     return lax.broadcasted_iota(jnp.int32, shape, axis)
 
 
+def quotient(x, size):
+    if size & (size - 1):
+        return lax.div(x, size)
+    return jnp.right_shift(x, size.bit_length() - 1)
+
+
+def remainder(x, size):
+    if size & (size - 1):
+        return lax.rem(x, size)
+    return jnp.bitwise_and(x, size - 1)
+
+
 def one_hot(hit):
     return jnp.where(hit, 1.0, 0.0).astype(jnp.bfloat16)
 
@@ -161,11 +173,15 @@
 def dense_kernel(
     peers,
     chunks,
-    params,
+    band_offset,
+    shift_frac,
     basis_ids,
+    basis_coef,
     widths,
-    image,
-    target,
+    image_hbm,
+    weights,
+    box_owner,
+    box_slot,
     template_out,
     diff_out,
     col_pass,
@@ -190,6 +206,9 @@
     recv2,
     gathered,
     matched,
+    image,
+    template_wide,
+    image_sem,
     weight_sems,
     sems0,
     sems1,
@@ -200,6 +219,8 @@
     f32 = jnp.float32
     depth = peers // 4
     rows, cols = image.shape[1:]
+    load = pltpu.make_async_copy(image_hbm, image, image_sem)
+    load.start()
     box_rows, box_cols = rows // BH, cols // BW
     boxes = box_rows * box_cols
     slots = peers * PS
@@ -229,20 +250,21 @@
             pl.semaphore_signal(barrier, inc=1, device_id=block_at(q), device_id_type=MESH)
 
     row_id = iota((slots, boxes), 0)
-    block = lax.div(row_id, PS)
-    a = lax.div(block, 2 * depth)
-    b = lax.rem(lax.div(block, depth), 2)
-    d = lax.rem(block, depth)
+    block = quotient(row_id, PS)
+    a = quotient(block, 2 * depth)
+    b = remainder(quotient(block, depth), 2)
+    d = remainder(block, depth)
     owner = (
-        lax.rem(layer + d, depth) * 2 + lax.rem(side + 1 - b, 2)
-    ) * 2 + lax.rem(core + 1 - a, 2)
-    hits = one_hot(owner * PS + lax.rem(row_id, PS) == target[...])
+        remainder(layer + d, depth) * 2 + remainder(side + 1 - b, 2)
+    ) * 2 + remainder(core + 1 - a, 2)
+    target = box_owner[...] * PS + box_slot[...]
+    hits = one_hot(owner * PS + remainder(row_id, PS) == target)
     k_row = iota((boxes, boxes), 0)
     k_col = iota((boxes, boxes), 1)
-    order_of = lambda k: lax.rem(k, box_rows) * box_cols + lax.div(k, box_rows)
+    order_of = lambda k: remainder(k, box_rows) * box_cols + quotient(k, box_rows)
     sorter = one_hot(k_row == order_of(k_col))
     sorter_t = one_hot(order_of(k_row) == k_col)
-    visit_weight = params[0, 2]
+    visit_weight = weights[...].astype(f32)
     tags = dot32(hits, sorter) * visit_weight
     tag_rows[...] = tags.astype(bf16)
     pick_rows[...] = lax.dot_general(
@@ -258,20 +280,20 @@
     half = BW // 2
     window = 2 * BW
     lane = iota((8, window), 1)
-    col_taps = lanczos_of((window - half - lane).astype(f32) - params[0, 1])
+    col_taps = lanczos_of((window - half - lane).astype(f32) - (band_offset[0, 1].astype(f32) + shift_frac[0, 1]))
     col_table = pltpu.roll(
         jnp.broadcast_to(col_taps[:1], (window, window)), 0, 1, stride=1, stride_axis=0
     )[:, :BW].astype(bf16)
     lane = iota((8, rows), 1)
     gap = jnp.where(lane < rows // 2, lane, lane - rows)
-    row_taps = lanczos_of(gap.astype(f32) - params[0, 0])
+    row_taps = lanczos_of(gap.astype(f32) - (band_offset[0, 0].astype(f32) + shift_frac[0, 0]))
     row_table = pltpu.roll(
         jnp.broadcast_to(row_taps[:1], (rows, rows)), 0, 1, stride=1, stride_axis=0
     )
     i_row = iota((rows, rows), 0)
     i_col = iota((rows, rows), 1)
     row_table = jnp.where(jnp.abs(i_col - i_row) < rows // 2, row_table, 0.0).astype(bf16)
-    place = lambda r: lax.rem(r, box_rows) * BH + lax.div(r, box_rows)
+    place = lambda r: remainder(r, box_rows) * BH + quotient(r, box_rows)
     row_warp[...] = dot32(one_hot(place(i_row) == i_col), row_table).astype(bf16)
 
     def windows(picture):
@@ -281,6 +303,7 @@
             [padded[:, j * BW : j * BW + window] for j in range(box_cols)], axis=0
         )
 
+    load.wait()
     step = rows // 4
     for part in range(4):
         here = slice(part * step, (part + 1) * step)
@@ -433,12 +456,14 @@
         near_first = [1]
     for ch in range(chunks):
         block = (close_chunk(0, ch) / wide_sum).astype(bf16)
-        template_out[:, ch * width : (ch + 1) * width] = block
         gathered[ch, own] = block
         for d in range(1, depth):
             along_z(ch, d).start()
         along_y(ch, 0).start()
         along_core(ch, depth).start()
+        for r in range(per):
+            template_wide[:, ch * per + r, :] = block[:, r * BW : (r + 1) * BW].astype(f32)
+    template_out[...] = template_wide[...].astype(bf16)
     for ch in range(chunks):
         for e in near_first:
             along_z(ch, depth - e).wait_recv()
@@ -480,7 +505,7 @@
     for j in range(0, cols, window):
         total = jnp.zeros((rows, window), f32)
         for member in range(members):
-            total = total + params[0, 3 + member] * dot32(
+            total = total + basis_coef[0, member] * dot32(
                 down_all[member], blurred[member, :, j : j + window]
             )
         matched[:, j : j + window] = (warped[:, j : j + window].astype(f32) - total).astype(bf16)
@@ -489,7 +514,9 @@
         open_chunk(1, ch, matched[ch * band_rows : (ch + 1) * band_rows, :])
     middle(1)
     for ch in range(chunks):
-        diff_out[:, ch * width : (ch + 1) * width] = close_chunk(1, ch) / wide_sum
+        block = close_chunk(1, ch) / wide_sum
+        for r in range(per):
+            diff_out[:, ch * per + r, :] = block[:, r * BW : (r + 1) * BW]
 
     finish(0)
     finish(1)
@@ -526,25 +553,16 @@
     chunks = CHUNKS
     width = BH * BW // chunks
     bf16, f32 = jnp.bfloat16, jnp.float32
-    params = jnp.concatenate(
-        [
-            band_offset.astype(f32) + shift_frac,
-            weights.astype(f32)[None, :],
-            basis_coef,
-        ],
-        axis=1,
-    )
-    target = box_owner[:, :, 0] * PS + box_slot
     smem = pl.BlockSpec(memory_space=pltpu.SMEM)
     vmem = pl.BlockSpec(memory_space=pltpu.VMEM)
     dma = pltpu.SemaphoreType.DMA
-    template, difference = pl.pallas_call(
+    return pl.pallas_call(
         functools.partial(dense_kernel, peers, chunks),
         out_shape=(
-            jax.ShapeDtypeStruct((PS, BH * BW), bf16),
-            jax.ShapeDtypeStruct((PS, BH * BW), f32),
+            jax.ShapeDtypeStruct((PS, BH, BW), bf16),
+            jax.ShapeDtypeStruct((PS, BH, BW), f32),
         ),
-        in_specs=[smem, smem, smem, vmem, vmem],
+        in_specs=[smem] * 5 + [pl.BlockSpec(memory_space=pl.ANY), vmem, vmem, vmem],
         out_specs=(vmem, vmem),
         scratch_shapes=[
             pltpu.VMEM((rows, cols), bf16),
@@ -569,6 +587,9 @@
             pltpu.VMEM((2, chunks, depth - 1, PS, width), bf16),
             pltpu.VMEM((chunks, peers, PS, width), bf16),
             pltpu.VMEM((rows, cols), bf16),
+            pltpu.VMEM((1, rows, cols), bf16),
+            pltpu.VMEM((PS, BH, BW), f32),
+            dma,
             dma((2, peers)),
             dma((2, 2, chunks)),
             dma((2, 2, chunks)),
@@ -576,8 +597,17 @@
             dma((2, chunks, 4 * depth)),
         ],
         compiler_params=pltpu.CompilerParams(collective_id=0, has_side_effects=True),
-    )(params, basis_index, basis_width, visit_image, target)
-    return (template.reshape(PS, BH, BW), difference.reshape(PS, BH, BW))
+    )(
+        band_offset,
+        shift_frac,
+        basis_index,
+        basis_coef,
+        basis_width,
+        visit_image,
+        weights.reshape(1, 1),
+        box_owner.reshape(1, boxes),
+        box_slot,
+    )
 
 
 def any_shards(*arrays):

time: 54.5 us -> 51.5 us (0.945)
  local copies, waits for them, and re-layouts: 3.58 us -> 2.17 us
  other arithmetic: 1.1 us -> 0 us
    unnamed x14 -> x4, local copies, waits for them, and re-layouts: 3.58 us -> 2.17 us
    concatenate x1 -> x0, other arithmetic: 0.59 us -> none  [dense_shards(): jnp.concatenate([band_offset.astype(f32) + shift_frac, weights.astype(f32...]
where the time goes in v2:
time: 51.5 us; the launch traced here: 51.3 us
  Pallas kernels  47.9 us (93%)
  local copies, waits for them, and re-layouts  2.17 us (4%)
  between operations  1.3 us (3%)
    pallas_call x1, Pallas kernels, dense_shards(): pl.pallas_call(functools.partial(dense_kernel, peers, chunks), out_shape=...  47.9 us
    unnamed x4, local copies, waits for them, and re-layouts  2.17 us

profile of v2, /device:TPU:0, one launch (start us, length us, event | category | flops | bytes accessed | tf_op | source)
XLA Modules:
  0.0 51.3 jit_solution(2450377948392677680)
XLA Ops:
  1.3 47.9 %shard_map.104 = (bf16[16,16,128]{2,1,0:T(8,128)(2,1)}, f32[16,16,128]{2,1,0:T(8,128)}) custom-call(s32[1,2]{1,0:T(1,128)} %band_offset.1, f32[1,2]{1,0:T(1,128)} %shift_frac.1, s32[1,6]{1,0:T(1,128)} %basis_ids.1, f32[1,6]{1,0:T(1,128)} %basis_coef.1, f32[12]{0:T(128)} %widths.1, bf16[1,256,1024]{2,1,0:T(8,128)(2,1)} %image_hbm.1, ...), custom_call_target="tpu_custom_call" | custom-call | tf_op jit(solution)/shard_map/pallas_call | solution.py:559
  49.1 0.0 copy-start
  49.2 1.5 %copy.14 = bf16[16,16,128]{2,1,0:T(8,128)(2,1)} copy(bf16[16,16,128]{2,1,0:T(8,128)(2,1)} %get-tuple-element.4) | data formatting | bytes 131072
  50.7 0.0 copy-done
  50.7 0.7 %copy.15 = f32[16,16,128]{2,1,0:T(8,128)} copy(f32[16,16,128]{2,1,0:T(8,128)S(1)} %copy-done) | data formatting | bytes 262144
Async XLA Ops:
  49.1 1.5 %copy-start = (f32[16,16,128]{2,1,0:T(8,128)S(1)}, f32[16,16,128]{2,1,0:T(8,128)}, u32[]{:S(2)}) copy-start(f32[16,16,128]{2,1,0:T(8,128)} %get-tuple-element.5) | copy-start | bytes 393220

commit v3 on v2

--- a/solution.py
+++ b/solution.py
@@ -207,7 +207,6 @@
     gathered,
     matched,
     image,
-    template_wide,
     image_sem,
     weight_sems,
     sems0,
@@ -454,6 +453,14 @@
     near_first = [e for e in (1, depth - 1)] + [e for e in range(2, depth - 1)]
     if depth == 2:
         near_first = [1]
+    def pass_on(ch):
+        along_y(ch, 0).wait_recv()
+        along_core(ch, 0).start()
+        for e in near_first:
+            along_z(ch, depth - e).wait_recv()
+            along_y(ch, e).start()
+            along_core(ch, depth + e).start()
+
     for ch in range(chunks):
         block = (close_chunk(0, ch) / wide_sum).astype(bf16)
         gathered[ch, own] = block
@@ -462,15 +469,11 @@
         along_y(ch, 0).start()
         along_core(ch, depth).start()
         for r in range(per):
-            template_wide[:, ch * per + r, :] = block[:, r * BW : (r + 1) * BW].astype(f32)
-    template_out[...] = template_wide[...].astype(bf16)
-    for ch in range(chunks):
-        for e in near_first:
-            along_z(ch, depth - e).wait_recv()
-            along_y(ch, e).start()
-            along_core(ch, depth + e).start()
-        along_y(ch, 0).wait_recv()
-        along_core(ch, 0).start()
+            template_out[:, ch * per + r, :] = block[:, r * BW : (r + 1) * BW].astype(f32)
+        if ch >= 2:
+            pass_on(ch - 2)
+    for ch in range(max(0, chunks - 2), chunks):
+        pass_on(ch)
     for ch in range(chunks):
         for e in near_first:
             along_y(ch, e).wait_recv()
@@ -556,10 +559,10 @@
     smem = pl.BlockSpec(memory_space=pltpu.SMEM)
     vmem = pl.BlockSpec(memory_space=pltpu.VMEM)
     dma = pltpu.SemaphoreType.DMA
-    return pl.pallas_call(
+    template, difference = pl.pallas_call(
         functools.partial(dense_kernel, peers, chunks),
         out_shape=(
-            jax.ShapeDtypeStruct((PS, BH, BW), bf16),
+            jax.ShapeDtypeStruct((PS, BH, BW), f32),
             jax.ShapeDtypeStruct((PS, BH, BW), f32),
         ),
         in_specs=[smem] * 5 + [pl.BlockSpec(memory_space=pl.ANY), vmem, vmem, vmem],
@@ -588,7 +591,6 @@
             pltpu.VMEM((chunks, peers, PS, width), bf16),
             pltpu.VMEM((rows, cols), bf16),
             pltpu.VMEM((1, rows, cols), bf16),
-            pltpu.VMEM((PS, BH, BW), f32),
             dma,
             dma((2, peers)),
             dma((2, 2, chunks)),
@@ -608,6 +610,7 @@
         box_owner.reshape(1, boxes),
         box_slot,
     )
+    return template.astype(bf16), difference
 
 
 def any_shards(*arrays):

time: 51.5 us -> 52.6 us (1.021)
  other arithmetic: 0 us -> 1.58 us
  local copies, waits for them, and re-layouts: 2.17 us -> 0.66 us
  Pallas kernels: 47.9 us -> 48.9 us
    convert_element_type x0 -> x1, other arithmetic: none -> 1.58 us  [dense_shards(): return (template.astype(bf16), difference)]
    unnamed x4 -> x3, local copies, waits for them, and re-layouts: 2.17 us -> 0.66 us
    pallas_call x1, Pallas kernels: 47.9 us -> 48.9 us  [dense_shards(): pl.pallas_call(functools.partial(dense_kernel, peers, chunks), out_shape=...]
where the time goes in v3:
time: 52.6 us; the launch traced here: 52.4 us
  Pallas kernels  48.9 us (93%)
  other arithmetic  1.58 us (3%)
  between operations  1.3 us (2%)
  local copies, waits for them, and re-layouts  0.66 us (1%)
    pallas_call x1, Pallas kernels, dense_shards(): pl.pallas_call(functools.partial(dense_kernel, peers, chunks), out_shape=...  48.9 us
    convert_element_type x1, other arithmetic, dense_shards(): return (template.astype(bf16), difference)  1.58 us

profile of v3, /device:TPU:0, one launch (start us, length us, event | category | flops | bytes accessed | tf_op | source)
XLA Modules:
  0.0 52.4 jit_solution(3832225592824556937)
XLA Ops:
  1.3 48.9 %shard_map.104 = (f32[16,16,128]{2,1,0:T(8,128)}, f32[16,16,128]{2,1,0:T(8,128)}) custom-call(s32[1,2]{1,0:T(1,128)} %band_offset.1, f32[1,2]{1,0:T(1,128)} %shift_frac.1, s32[1,6]{1,0:T(1,128)} %basis_ids.1, f32[1,6]{1,0:T(1,128)} %basis_coef.1, f32[12]{0:T(128)} %widths.1, bf16[1,256,1024]{2,1,0:T(8,128)(2,1)} %image_hbm.1, bf16[1,1]{1,0:T(2,128)(2,1)} %bitcast.2.weights, ...), custom_call_target="tpu_custom_call" | custom-call | tf_op jit(solution)/shard_map/pallas_call | solution.py:562
  50.2 0.0 copy-start
  50.2 1.6 %convert_element_type.3 = bf16[16,16,128]{2,1,0:T(8,128)(2,1)} convert(f32[16,16,128]{2,1,0:T(8,128)} %get-tuple-element.4) | non-fusion elementwise | flops 32768 | bytes 196608 | tf_op jit(solution)/shard_map/convert_element_type | solution.py:613
  51.8 0.0 copy-done
  51.8 0.7 %copy.13 = f32[16,16,128]{2,1,0:T(8,128)} copy(f32[16,16,128]{2,1,0:T(8,128)S(1)} %copy-done) | data formatting | bytes 262144
Async XLA Ops:
  50.2 1.6 %copy-start = (f32[16,16,128]{2,1,0:T(8,128)S(1)}, f32[16,16,128]{2,1,0:T(8,128)}, u32[]{:S(2)}) copy-start(f32[16,16,128]{2,1,0:T(8,128)} %get-tuple-element.9) | copy-start | bytes 393220

commit v4 on v2

--- a/solution.py
+++ b/solution.py
@@ -396,13 +396,13 @@
         )
 
     pl.semaphore_wait(barrier, peers - 1)
+    for ch in range(chunks):
+        here = slice(ch * band_rows, (ch + 1) * band_rows)
+        warped[here, :] = dot32(row_warp[here, :], col_pass[...]).astype(bf16)
+        open_chunk(0, ch, warped[here, :])
     for q in range(peers):
         if q != own:
             weight_copy(q).start()
-    for ch in range(chunks):
-        here = slice(ch * band_rows, (ch + 1) * band_rows)
-        warped[here, :] = dot32(row_warp[here, :], col_pass[...]).astype(bf16)
-        open_chunk(0, ch, warped[here, :])
 
     across_gap = (iota((window, BW), 0) - iota((window, BW), 1) - half).astype(f32)
     down_gap = (place(i_row) - place(i_col)).astype(f32)

time: 51.5 us -> 52.3 us (1.016)
  Pallas kernels: 47.9 us -> 48.6 us
    pallas_call x1, Pallas kernels: 47.9 us -> 48.6 us  [dense_shards(): pl.pallas_call(functools.partial(dense_kernel, peers, chunks), out_shape=...]
where the time goes in v4:
time: 52.3 us; the launch traced here: 52.1 us
  Pallas kernels  48.6 us (93%)
  local copies, waits for them, and re-layouts  2.17 us (4%)
  between operations  1.3 us (2%)
    pallas_call x1, Pallas kernels, dense_shards(): pl.pallas_call(functools.partial(dense_kernel, peers, chunks), out_shape=...  48.6 us
    unnamed x4, local copies, waits for them, and re-layouts  2.17 us

profile of v4, /device:TPU:0, one launch (start us, length us, event | category | flops | bytes accessed | tf_op | source)
XLA Modules:
  0.0 52.1 jit_solution(3787411906583721244)
XLA Ops:
  1.3 48.6 %shard_map.104 = (bf16[16,16,128]{2,1,0:T(8,128)(2,1)}, f32[16,16,128]{2,1,0:T(8,128)}) custom-call(s32[1,2]{1,0:T(1,128)} %band_offset.1, f32[1,2]{1,0:T(1,128)} %shift_frac.1, s32[1,6]{1,0:T(1,128)} %basis_ids.1, f32[1,6]{1,0:T(1,128)} %basis_coef.1, f32[12]{0:T(128)} %widths.1, bf16[1,256,1024]{2,1,0:T(8,128)(2,1)} %image_hbm.1, ...), custom_call_target="tpu_custom_call" | custom-call | tf_op jit(solution)/shard_map/pallas_call | solution.py:559
  49.9 0.0 copy-start
  49.9 1.5 %copy.14 = bf16[16,16,128]{2,1,0:T(8,128)(2,1)} copy(bf16[16,16,128]{2,1,0:T(8,128)(2,1)} %get-tuple-element.4) | data formatting | bytes 131072
  51.4 0.0 copy-done
  51.4 0.7 %copy.15 = f32[16,16,128]{2,1,0:T(8,128)} copy(f32[16,16,128]{2,1,0:T(8,128)S(1)} %copy-done) | data formatting | bytes 262144
Async XLA Ops:
  49.9 1.5 %copy-start = (f32[16,16,128]{2,1,0:T(8,128)S(1)}, f32[16,16,128]{2,1,0:T(8,128)}, u32[]{:S(2)}) copy-start(f32[16,16,128]{2,1,0:T(8,128)} %get-tuple-element.5) | copy-start | bytes 393220
